TPU v7x, 32 devices: a whole 2x2x4 slice. The times are simulated.
32 devices in a mesh: rep: 4 (over y, x), fsdp: 4 (over z), ctx: 2 (over core).
Axes of the slice: x: 2, y: 2, z: 4, core: 2. Of those that a mesh axis runs over, the one named last changes fastest.
Arguments:
- inputs: bfloat16 [2, 16, 1024, 768], P(None, ('rep', 'fsdp'), 'ctx'), may hold values from -6 to 6
- weight_qkv: bfloat16 [768, 2304], P('fsdp'), may hold values from -0.21875 to 0.21875
- bias_query: bfloat16 [768], P('fsdp'), may hold values from -3 to 3
- bias_value: bfloat16 [768], P('fsdp'), may hold values from -3 to 3
- weight_mix: bfloat16 [768, 768], P('fsdp'), may hold values from -1.75 to 1.75
- bias_mix: bfloat16 [768], P('fsdp'), may hold values from -2 to 2
- gain_attn: bfloat16 [768], P('fsdp'), may hold values from 0.099609375 to 1.8984375
- shift_attn: bfloat16 [768], P('fsdp'), may hold values from -2 to 2
- gain_mlp: bfloat16 [768], P('fsdp'), may hold values from 0.099609375 to 1.8984375
- shift_mlp: bfloat16 [768], P('fsdp'), may hold values from -2 to 2
- weight_up: bfloat16 [768, 3072], P('fsdp'), may hold values from -0.21875 to 0.21875
- bias_up: bfloat16 [3072], P('fsdp'), may hold values from -3 to 3
- weight_down: bfloat16 [3072, 768], P('fsdp'), may hold values from -0.109375 to 0.109375
- bias_down: bfloat16 [768], P('fsdp'), may hold values from -2 to 2
- cotangent: bfloat16 [2, 16, 1024, 768], P(None, ('rep', 'fsdp'), 'ctx'), may hold values from -6 to 6
Outputs:
- outputs: bfloat16 [2, 16, 1024, 768], P(None, ('rep', 'fsdp'), 'ctx')
- grad_inputs: float32 [2, 16, 1024, 768], P(None, ('rep', 'fsdp'), 'ctx')
- weight_qkv_grad: float32 [768, 2304], P('fsdp')
- bias_query_grad: float32 [768], P('fsdp')
- bias_value_grad: float32 [768], P('fsdp')
- weight_mix_grad: float32 [768, 768], P('fsdp')
- bias_mix_grad: float32 [768], P('fsdp')
- gain_attn_grad: float32 [768], P('fsdp')
- shift_attn_grad: float32 [768], P('fsdp')
- gain_mlp_grad: float32 [768], P('fsdp')
- shift_mlp_grad: float32 [768], P('fsdp')
- weight_up_grad: float32 [768, 3072], P('fsdp')
- bias_up_grad: float32 [3072], P('fsdp')
- weight_down_grad: float32 [3072, 768], P('fsdp')
- bias_down_grad: float32 [768], P('fsdp')
All inputs are finite; a program needn't handle non-finite values.
Results may differ from a plain program's by a relative error of at most 0.018.
Values may be sent and summed in bfloat16 or wider, within the bound.
A program may use at most 320 MiB of HBM per device.

v0:
```python
from functools import partial
import jax
import jax.numpy as jnp
from jax import lax
from jax.sharding import PartitionSpec as P

H = 12
EPS = 1e-05


def from_behind(x, axis, by):
    peers = lax.axis_size(axis)
    pairs = [(i, i + by) for i in range(peers) if 0 <= i + by < peers]
    return lax.ppermute(x, axis, pairs)


def for_sending(x):

    def short(part):
        return part.astype(jnp.bfloat16) if part.dtype == jnp.float32 else part

    return jax.tree.map(short, x)


def norm_stats(values):
    center = values - jnp.mean(values, axis=-1, keepdims=True)
    inverse = lax.rsqrt(jnp.mean(center * center, axis=-1, keepdims=True) + EPS)
    return (center * inverse, inverse)


def norm_back(grad_norm, normal, inverse, gain):
    scaled = grad_norm * gain
    return inverse * (
        scaled
        - jnp.mean(scaled, axis=-1, keepdims=True)
        - normal * jnp.mean(scaled * normal, axis=-1, keepdims=True)
    )


def column_sum(values):
    return jnp.sum(values.astype(jnp.float32), axis=(0, 1))


def outer_sum(left, right):
    return jnp.einsum("sri,srj->ij", left, right, preferred_element_type=jnp.float32)


def project(left, weight):
    return jnp.einsum("sri,ij->srj", left, weight, preferred_element_type=jnp.float32)


def project_back(grad_rows, weight):
    return jnp.einsum("srj,ij->sri", grad_rows, weight, preferred_element_type=jnp.float32)


def split_heads(values):
    return values.reshape(values.shape[0], values.shape[1], H, values.shape[2] // H)


def attention_scores(query_heads, key_heads, allowed, factor):
    raw = jnp.einsum("sqhd,skhd->shqk", query_heads, key_heads, preferred_element_type=jnp.float32)
    return jnp.where(allowed, raw * factor, -1e30)


def local(
    inputs,
    weight_qkv,
    bias_query,
    bias_value,
    weight_mix,
    bias_mix,
    gain_attn,
    shift_attn,
    gain_mlp,
    shift_mlp,
    weight_up,
    bias_up,
    weight_down,
    bias_down,
    cotangent,
):
    shards = (
        weight_qkv,
        bias_query,
        bias_value,
        weight_mix,
        bias_mix,
        gain_attn,
        shift_attn,
        gain_mlp,
        shift_mlp,
        weight_up,
        bias_up,
        weight_down,
        bias_down,
    )
    width = weight_qkv.shape[1] // 3
    factor = (width // H) ** (-0.5)
    rows = inputs.shape[2]
    owners = lax.axis_size("fsdp")
    ctx_index = lax.axis_index("ctx")
    query_pos = lax.broadcasted_iota(jnp.int32, (rows, 2 * rows), 0)
    key_pos = lax.broadcasted_iota(jnp.int32, (rows, 2 * rows), 1) - rows
    allowed = (key_pos <= query_pos) & ((key_pos >= 0) | (ctx_index > 0))
    whole_zeros = tuple(
        (jnp.zeros((item.shape[0] * owners,) + item.shape[1:], jnp.float32) for item in shards)
    )
    bf16 = jnp.bfloat16
    f32 = jnp.float32

    def micro(totals, pair):
        tokens_in, grad_in = pair
        full = (
            lax.all_gather(shards[0], "fsdp", axis=0, tiled=True),
            lax.all_gather(shards[1], "fsdp", axis=0, tiled=True),
            lax.all_gather(shards[2], "fsdp", axis=0, tiled=True),
            lax.all_gather(shards[3], "fsdp", axis=0, tiled=True),
            lax.all_gather(shards[4], "fsdp", axis=0, tiled=True),
            lax.all_gather(shards[5], "fsdp", axis=0, tiled=True),
            lax.all_gather(shards[6], "fsdp", axis=0, tiled=True),
            lax.all_gather(shards[7], "fsdp", axis=0, tiled=True),
            lax.all_gather(shards[8], "fsdp", axis=0, tiled=True),
            lax.all_gather(shards[9], "fsdp", axis=0, tiled=True),
            lax.all_gather(shards[10], "fsdp", axis=0, tiled=True),
            lax.all_gather(shards[11], "fsdp", axis=0, tiled=True),
            lax.all_gather(shards[12], "fsdp", axis=0, tiled=True),
        )
        tokens = tokens_in.astype(f32)
        normal_one, inverse_one = norm_stats(tokens)
        first = (normal_one * full[5] + full[6]).astype(bf16)
        joined = project(first, full[0])
        query = (joined[..., :width] + full[1]).astype(bf16)
        key_own = joined[..., width : 2 * width].astype(bf16)
        value_own = (joined[..., 2 * width :] + full[2]).astype(bf16)
        key_prev, value_prev = from_behind((key_own, value_own), "ctx", 1)
        key_heads = split_heads(jnp.concatenate([key_prev, key_own], axis=1))
        value_heads = split_heads(jnp.concatenate([value_prev, value_own], axis=1))
        query_heads = split_heads(query)
        scores = attention_scores(query_heads, key_heads, allowed, factor)
        top = jnp.max(scores, axis=-1, keepdims=True)
        logsum = top + jnp.log(jnp.sum(jnp.exp(scores - top), axis=-1, keepdims=True))
        probs_low = jnp.exp(scores - logsum).astype(bf16)
        mixed = jnp.einsum("shqk,skhd->sqhd", probs_low, value_heads, preferred_element_type=f32)
        mixed = mixed.reshape(tokens.shape).astype(bf16)
        middle = tokens + project(mixed, full[3]) + full[4]
        normal_two, inverse_two = norm_stats(middle)
        second = (normal_two * full[7] + full[8]).astype(bf16)
        before = project(second, full[9]) + full[10]
        active = jax.nn.gelu(before, approximate=True).astype(bf16)
        result = (middle + project(active, full[11]) + full[12]).astype(bf16)
        again = (
            lax.all_gather(shards[0], "fsdp", axis=0, tiled=True),
            lax.all_gather(shards[1], "fsdp", axis=0, tiled=True),
            lax.all_gather(shards[2], "fsdp", axis=0, tiled=True),
            lax.all_gather(shards[3], "fsdp", axis=0, tiled=True),
            lax.all_gather(shards[4], "fsdp", axis=0, tiled=True),
            lax.all_gather(shards[5], "fsdp", axis=0, tiled=True),
            lax.all_gather(shards[6], "fsdp", axis=0, tiled=True),
            lax.all_gather(shards[7], "fsdp", axis=0, tiled=True),
            lax.all_gather(shards[8], "fsdp", axis=0, tiled=True),
            lax.all_gather(shards[9], "fsdp", axis=0, tiled=True),
            lax.all_gather(shards[10], "fsdp", axis=0, tiled=True),
            lax.all_gather(shards[11], "fsdp", axis=0, tiled=True),
            lax.all_gather(shards[12], "fsdp", axis=0, tiled=True),
        )
        grad_out = grad_in.astype(f32)
        d_down = grad_out.astype(bf16)
        g_wdown = outer_sum(active, d_down)
        g_bdown = column_sum(d_down)
        d_active = project_back(d_down, again[11])
        gelu_back = jax.vjp(partial(jax.nn.gelu, approximate=True), before)[1]
        d_before = gelu_back(d_active)[0].astype(bf16)
        g_wup = outer_sum(second, d_before)
        g_bup = column_sum(d_before)
        d_second = project_back(d_before, again[9])
        g_gmlp = jnp.sum(d_second * normal_two, axis=(0, 1))
        g_smlp = jnp.sum(d_second, axis=(0, 1))
        d_middle = grad_out + norm_back(d_second, normal_two, inverse_two, again[7])
        d_branch = d_middle.astype(bf16)
        g_wmix = outer_sum(mixed, d_branch)
        g_bmix = column_sum(d_branch)
        d_mixed = split_heads(project_back(d_branch, again[3]).astype(bf16))
        scores = attention_scores(query_heads, key_heads, allowed, factor)
        probs = jnp.exp(scores - logsum)
        probs_low = probs.astype(bf16)
        d_probs = jnp.einsum("sqhd,skhd->shqk", d_mixed, value_heads, preferred_element_type=f32)
        d_scores = (
            probs * (d_probs - jnp.sum(d_probs * probs, axis=-1, keepdims=True)) * factor
        ).astype(bf16)
        d_query = jnp.einsum("shqk,skhd->sqhd", d_scores, key_heads, preferred_element_type=f32)
        d_query = d_query.reshape(tokens.shape).astype(bf16)
        d_key_all = jnp.einsum("shqk,sqhd->skhd", d_scores, query_heads, preferred_element_type=f32)
        d_value_all = jnp.einsum("shqk,sqhd->skhd", probs_low, d_mixed, preferred_element_type=f32)
        d_key_all = d_key_all.reshape(tokens.shape[0], 2 * rows, width)
        d_value_all = d_value_all.reshape(tokens.shape[0], 2 * rows, width)
        key_back, value_back = (
            from_behind(d_key_all[:, :rows].astype(jnp.bfloat16), "ctx", -1).astype(jnp.float32),
            from_behind(d_value_all[:, :rows].astype(jnp.bfloat16), "ctx", -1).astype(jnp.float32),
        )
        d_key = (d_key_all[:, rows:] + key_back).astype(bf16)
        d_value = (d_value_all[:, rows:] + value_back).astype(bf16)
        d_joined = jnp.concatenate([d_query, d_key, d_value], axis=-1)
        g_wqkv = outer_sum(first, d_joined)
        g_bquery = column_sum(d_query)
        g_bvalue = column_sum(d_value)
        d_first = project_back(d_joined, again[0])
        g_gattn = jnp.sum(d_first * normal_one, axis=(0, 1))
        g_sattn = jnp.sum(d_first, axis=(0, 1))
        d_tokens = d_middle + norm_back(d_first, normal_one, inverse_one, again[5])
        terms = (
            g_wqkv,
            g_bquery,
            g_bvalue,
            g_wmix,
            g_bmix,
            g_gattn,
            g_sattn,
            g_gmlp,
            g_smlp,
            g_wup,
            g_bup,
            g_wdown,
            g_bdown,
        )
        totals = tuple((left + right for left, right in zip(totals, terms)))
        return (totals, (result, d_tokens))

    totals, (results, grad_tokens) = lax.scan(micro, whole_zeros, (inputs, cotangent))
    shares = jax.tree.map(
        lambda part: part.astype(jnp.float32),
        lax.psum_scatter(for_sending(totals), "fsdp", scatter_dimension=0, tiled=True),
    )
    summed = jax.tree.map(
        lambda part: part.astype(jnp.float32), lax.psum(for_sending(shares), ("rep", "ctx"))
    )
    return (results, grad_tokens) + tuple(summed)


def solution(mesh):
    in_specs = (
        P(None, ("rep", "fsdp"), "ctx", None),
        P("fsdp", None),
        P("fsdp"),
        P("fsdp"),
        P("fsdp", None),
        P("fsdp"),
        P("fsdp"),
        P("fsdp"),
        P("fsdp"),
        P("fsdp"),
        P("fsdp", None),
        P("fsdp"),
        P("fsdp", None),
        P("fsdp"),
        P(None, ("rep", "fsdp"), "ctx", None),
    )
    out_specs = (
        P(None, ("rep", "fsdp"), "ctx", None),
        P(None, ("rep", "fsdp"), "ctx", None),
        P("fsdp", None),
        P("fsdp"),
        P("fsdp"),
        P("fsdp", None),
        P("fsdp"),
        P("fsdp"),
        P("fsdp"),
        P("fsdp"),
        P("fsdp"),
        P("fsdp", None),
        P("fsdp"),
        P("fsdp", None),
        P("fsdp"),
    )
    return jax.shard_map(local, mesh=mesh, in_specs=in_specs, out_specs=out_specs, check_vma=False)
```

profile of v0, /device:TPU:0, one launch (start us, length us, event | category | flops | bytes accessed | tf_op | source)
XLA Modules:
  0.0 1352.4 jit_solution(5778753269937234375)
XLA Ops:
  8.2 974.8 %while.41 = (s32[]{:T(128)}, f32[768,2304]{1,0:T(8,128)}, f32[768]{0:T(1024)}, f32[768]{0:T(1024)}, f32[768,768]{1,0:T(8,128)}, /*index=5*/f32[768]{0:T(1024)}, ...) while((s32[]{:T(128)}, f32[768,2304]{1,0:T(8,128)}, ...), condition=%wide.region_21.22_spmd.clone, body=%wide.region_0.21_spmd.clone.sunk | while | flops 26950144000 | bytes 699213696 | solution.py:228
  19.6 21.4 %all-reduce.30 = (bf16[768]{0:T(1024)(128)(2,1)S(1)}, bf16[768]{0:T(1024)(128)(2,1)S(1)}, bf16[768]{0:T(1024)(128)(2,1)S(1)}, bf16[768]{0:T(1024)(128)(2,1)S(1)}...) all-reduce(bf16[768]{0:T(1024)(128)(2,1)S(1)} %dynamic-update-slice, ...), channel_id=1, replica_groups=mesh['rep'=4,'fsdp'=4,'ctx'=2] {'fsdp'}, use_global_device_ids=true, to_apply=%add.1 | all-reduce | flops 6144 | bytes 24576 | tf_op jit(solution)/shard_map/while
  42.7 41.6 %all-gather.11.cloned.1.call-done = bf16[768,2304]{1,0:T(8,128)(2,1)} async-done(((bf16[192,2304]{1,0:T(8,128)(2,1)}), bf16[768,2304]{1,0:T(8,128)(2,1)}) %all-gather.11.cloned.1.call-update) | async-done | bytes 3538960 | tf_op jit(solution)/shard_map/while/body/eval_jaxpr/all_gather | solution.py:114
  84.3 4.2 convolution_bitcast_fusion.2
  88.8 2.7 collective-permute-start
  94.7 13.2 all-gather.3
  116.7 15.2 %fusion.201 = (f32[12,512]{1,0:T(8,128)S(1)}, f32[12,512,1024]{2,1,0:T(8,128)}) fusion(pred[512,1024]{1,0:T(8,128)(4,1)} %fusion.200, bf16[512,12,64]{0,2,1:T(8,128)(2,1)} %bitcast.212, bf16[1024,12,64]{0,2,1:T(8,128)(2,1)} %bitcast.210), kind=kOutput, calls=%fused_computation.8.clone.1 | convolution fusion | flops 824174592 | bytes 28073984 | tf_op jit(solution)/shard_map/while/body/eval_jaxpr/sqhd,skhd->shqk/dot_general | solution.py:61
  131.9 11.8 exponential_reduce_fusion.2
  143.8 12.1 convolution_convert_fusion.4
  155.9 2.7 fusion.202
  158.9 46.3 %all-gather.13.cloned.1.call-done = bf16[768,3072]{1,0:T(8,128)(2,1)} async-done(((bf16[192,3072]{1,0:T(8,128)(2,1)}), bf16[768,3072]{1,0:T(8,128)(2,1)}) %all-gather.13.cloned.1.call-update) | async-done | bytes 4718608 | tf_op jit(solution)/shard_map/while/body/eval_jaxpr/all_gather | solution.py:123
  205.2 7.1 fusion.203
  212.3 82.2 %all-gather.15.cloned.1.call-done = bf16[3072,768]{1,0:T(8,128)(2,1)} async-done(((bf16[768,768]{1,0:T(8,128)(2,1)}), bf16[3072,768]{1,0:T(8,128)(2,1)}) %all-gather.15.cloned.1.call-update) | async-done | bytes 4718608 | tf_op jit(solution)/shard_map/while/body/eval_jaxpr/all_gather | solution.py:163
  294.5 9.3 convert_reduce_fusion.13
  303.8 3.0 multiply_reduce_fusion.9
  309.9 2.3 copy.53
  312.2 13.6 %fusion.204 = f32[12,64,1024]{2,1,0:T(8,128)} fusion(bf16[512,12,64]{0,2,1:T(8,128)(2,1)} %bitcast.208, f32[12,512]{1,0:T(8,128)S(1)} %log_add_fusion.2, f32[12,512,1024]{2,1,0:T(8,128)} %get-tuple-element.914, pred[512,1024]{1,0:T(8,128)(4,1)} %fusion.200), kind=kOutput, calls=%fused_computation.107.clone.1 | convolution fusion | flops 830472192 | bytes 29646848 | tf_op jit(solution)/shard_map/while/body/eval_jaxpr/shqk,sqhd->skhd/dot_general | solution.py:193
  325.8 10.1 fusion.205
  335.9 52.3 %convert_reduce_fusion.16 = (f32[12,64]{1,0:T(8,128)S(1)}, bf16[12,64,512]{2,1,0:T(8,128)(2,1)}) fusion(bf16[1024,12,64]{0,2,1:T(8,128)(2,1)} %bitcast.211, f32[12,512,1024]{2,1,0:T(8,128)} %fusion.205, f32[12,512]{1,0:T(8,128)S(1)} %log_add_fusion.2, f32[12,512,1024]{2,1,0:T(8,128)} %get-tuple-element.914, pred[512,1024]{1,0:T(8,128)(4,1)} %fusion.200), kind=kOutput, calls=%fused_computation.77.clone.1 | convolution fusion | flops 875698432 | bytes 53242880 | tf_op jit(solution)/shard_map/while/body/eval_jaxpr/shqk,skhd->sqhd/dot_general | solution.py:190
  388.2 54.3 %fusion.206 = f32[12,64,1024]{2,1,0:T(8,128)} fusion(bf16[512,12,64]{0,2,1:T(8,128)(2,1)} %bitcast.213, f32[12,512,1024]{2,1,0:T(8,128)} %fusion.205, f32[12,512]{1,0:T(8,128)S(1)} %log_add_fusion.2, f32[12,512,1024]{2,1,0:T(8,128)} %get-tuple-element.914, pred[512,1024]{1,0:T(8,128)(4,1)} %fusion.200), kind=kOutput, calls=%fused_computation.10.clone.1 | convolution fusion | flops 874519552 | bytes 54812672 | tf_op jit(solution)/shard_map/while/body/eval_jaxpr/shqk,sqhd->skhd/dot_general | solution.py:192
  442.5 10.5 select_add_fusion.31
  453.0 2.4 slice.86
  456.7 5.6 select_add_fusion.29
  465.2 9.1 fusion.209
  476.3 2.5 convert_reduce_fusion.15
  479.5 7.3 select_add_fusion.23
  486.8 2.7 fusion.208
  502.7 16.6 %all-reduce.30 = (bf16[768]{0:T(1024)(128)(2,1)S(1)}, bf16[768]{0:T(1024)(128)(2,1)S(1)}, bf16[768]{0:T(1024)(128)(2,1)S(1)}, bf16[768]{0:T(1024)(128)(2,1)S(1)}...) all-reduce(bf16[768]{0:T(1024)(128)(2,1)S(1)} %dynamic-update-slice, ...), channel_id=1, replica_groups=mesh['rep'=4,'fsdp'=4,'ctx'=2] {'fsdp'}, use_global_device_ids=true, to_apply=%add.1 | all-reduce | flops 6144 | bytes 24576 | tf_op jit(solution)/shard_map/while
  521.0 43.7 %all-gather.11.cloned.1.call-done = bf16[768,2304]{1,0:T(8,128)(2,1)} async-done(((bf16[192,2304]{1,0:T(8,128)(2,1)}), bf16[768,2304]{1,0:T(8,128)(2,1)}) %all-gather.11.cloned.1.call-update) | async-done | bytes 3538960 | tf_op jit(solution)/shard_map/while/body/eval_jaxpr/all_gather | solution.py:114
  564.6 4.1 convolution_bitcast_fusion.2
  569.1 2.8 collective-permute-start
  575.1 13.2 all-gather.3
  596.9 15.3 %fusion.201 = (f32[12,512]{1,0:T(8,128)S(1)}, f32[12,512,1024]{2,1,0:T(8,128)}) fusion(pred[512,1024]{1,0:T(8,128)(4,1)} %fusion.200, bf16[512,12,64]{0,2,1:T(8,128)(2,1)} %bitcast.212, bf16[1024,12,64]{0,2,1:T(8,128)(2,1)} %bitcast.210), kind=kOutput, calls=%fused_computation.8.clone.1 | convolution fusion | flops 824174592 | bytes 28073984 | tf_op jit(solution)/shard_map/while/body/eval_jaxpr/sqhd,skhd->shqk/dot_general | solution.py:61
  612.2 11.8 exponential_reduce_fusion.2
  624.0 12.1 convolution_convert_fusion.4
  636.1 2.7 fusion.202
  639.1 46.4 %all-gather.13.cloned.1.call-done = bf16[768,3072]{1,0:T(8,128)(2,1)} async-done(((bf16[192,3072]{1,0:T(8,128)(2,1)}), bf16[768,3072]{1,0:T(8,128)(2,1)}) %all-gather.13.cloned.1.call-update) | async-done | bytes 4718608 | tf_op jit(solution)/shard_map/while/body/eval_jaxpr/all_gather | solution.py:123
  685.5 7.1 fusion.203
  692.7 82.4 %all-gather.15.cloned.1.call-done = bf16[3072,768]{1,0:T(8,128)(2,1)} async-done(((bf16[768,768]{1,0:T(8,128)(2,1)}), bf16[3072,768]{1,0:T(8,128)(2,1)}) %all-gather.15.cloned.1.call-update) | async-done | bytes 4718608 | tf_op jit(solution)/shard_map/while/body/eval_jaxpr/all_gather | solution.py:163
  775.0 9.7 convert_reduce_fusion.13
  784.7 3.0 multiply_reduce_fusion.9
  793.1 13.6 %fusion.204 = f32[12,64,1024]{2,1,0:T(8,128)} fusion(bf16[512,12,64]{0,2,1:T(8,128)(2,1)} %bitcast.208, f32[12,512]{1,0:T(8,128)S(1)} %log_add_fusion.2, f32[12,512,1024]{2,1,0:T(8,128)} %get-tuple-element.914, pred[512,1024]{1,0:T(8,128)(4,1)} %fusion.200), kind=kOutput, calls=%fused_computation.107.clone.1 | convolution fusion | flops 830472192 | bytes 29646848 | tf_op jit(solution)/shard_map/while/body/eval_jaxpr/shqk,sqhd->skhd/dot_general | solution.py:193
  806.7 10.1 fusion.205
  816.8 52.3 %convert_reduce_fusion.16 = (f32[12,64]{1,0:T(8,128)S(1)}, bf16[12,64,512]{2,1,0:T(8,128)(2,1)}) fusion(bf16[1024,12,64]{0,2,1:T(8,128)(2,1)} %bitcast.211, f32[12,512,1024]{2,1,0:T(8,128)} %fusion.205, f32[12,512]{1,0:T(8,128)S(1)} %log_add_fusion.2, f32[12,512,1024]{2,1,0:T(8,128)} %get-tuple-element.914, pred[512,1024]{1,0:T(8,128)(4,1)} %fusion.200), kind=kOutput, calls=%fused_computation.77.clone.1 | convolution fusion | flops 875698432 | bytes 53242880 | tf_op jit(solution)/shard_map/while/body/eval_jaxpr/shqk,skhd->sqhd/dot_general | solution.py:190
  869.1 54.1 %fusion.206 = f32[12,64,1024]{2,1,0:T(8,128)} fusion(bf16[512,12,64]{0,2,1:T(8,128)(2,1)} %bitcast.213, f32[12,512,1024]{2,1,0:T(8,128)} %fusion.205, f32[12,512]{1,0:T(8,128)S(1)} %log_add_fusion.2, f32[12,512,1024]{2,1,0:T(8,128)} %get-tuple-element.914, pred[512,1024]{1,0:T(8,128)(4,1)} %fusion.200), kind=kOutput, calls=%fused_computation.10.clone.1 | convolution fusion | flops 874519552 | bytes 54812672 | tf_op jit(solution)/shard_map/while/body/eval_jaxpr/shqk,sqhd->skhd/dot_general | solution.py:192
  923.2 13.2 select_add_fusion.31
  936.4 2.4 slice.86
  940.1 7.9 select_add_fusion.29
  950.9 9.1 fusion.209
  962.0 2.5 convert_reduce_fusion.15
  965.1 9.5 select_add_fusion.23
  974.7 2.7 fusion.208
  983.1 2.8 convert_element_type.440
  986.0 5.2 convert_element_type.434
  991.2 6.8 convert_element_type.452
  998.0 6.4 convert_element_type.456
  1004.5 11.2 reduce-scatter.7.cloned.1.call-done
  1015.7 67.2 %reduce-scatter.5.cloned.1.call-done = bf16[192,2304]{1,0:T(8,128)(2,1)} async-done(((bf16[768,2304]{1,0:T(8,128)(2,1)}), bf16[192,2304]{1,0:T(8,128)(2,1)}) %reduce-scatter.5.cloned.1.call-update) | async-done | bytes 884752 | tf_op jit(solution)/shard_map/reduce_scatter | solution.py:231
  1082.9 87.5 %reduce-scatter.9.cloned.1.call-done = bf16[192,3072]{1,0:T(8,128)(2,1)} async-done(((bf16[768,3072]{1,0:T(8,128)(2,1)}), bf16[192,3072]{1,0:T(8,128)(2,1)}) %reduce-scatter.9.cloned.1.call-update) | async-done | bytes 1179664 | tf_op jit(solution)/shard_map/reduce_scatter | solution.py:231
  1170.4 88.0 %reduce-scatter.11.cloned.1.call-done = bf16[768,768]{1,0:T(8,128)(2,1)} async-done(((bf16[3072,768]{1,0:T(8,128)(2,1)}), bf16[768,768]{1,0:T(8,128)(2,1)}) %reduce-scatter.11.cloned.1.call-update) | async-done | bytes 1179664 | tf_op jit(solution)/shard_map/reduce_scatter | solution.py:231
  1260.5 18.3 %all-reduce.28 = (bf16[768]{0:T(1024)(128)(2,1)S(1)}, bf16[768]{0:T(1024)(128)(2,1)S(1)}, bf16[768]{0:T(1024)(128)(2,1)S(1)}, bf16[768]{0:T(1024)(128)(2,1)S(1)}...) all-reduce(bf16[768]{0:T(1024)(128)(2,1)S(1)} %convert_element_type, ...), channel_id=3, replica_groups=mesh['rep'=4,'fsdp'=4,'ctx'=2] {'fsdp'}, use_global_device_ids=true, to_apply=%region_24.25.clone | all-reduce | flops 9216 | bytes 36864
  1279.5 12.3 all-reduce.26
  1296.9 40.1 %all-reduce.33.cloned.1.call-done = (bf16[192,2304]{1,0:T(8,128)(2,1)}, bf16[192,768]{1,0:T(8,128)(2,1)}, bf16[192,3072]{1,0:T(8,128)(2,1)}, bf16[768,768]{1,0:T(8,128)(2,1)}) async-done(((bf16[192,2304]{1,0:T(8,128)(2,1)}, bf16[192,768]{1,0:T(8,128)(2,1)}, bf16[192,3072]{1,0:T(8,128)(2,1)}, bf16[768,768]{1,0:T(8,128)(2,1)}), (bf16[192,2304]{1,0:T(8,128)(2,1)}, bf16[192,768]{1,0:T(8,128)(2,1)}, ...) | async-done | bytes 3538960 | tf_op jit(solution)/shard_map/psum | solution.py:234
  1338.8 2.6 convert_element_type.435
  (393 shorter events, 86.1 us)
Async XLA Ops:
  8.6 99.5 %copy-start.21 = (s32[1024]{0:T(1024)}, s32[1024]{0:T(1024)S(1)}, u32[]{:S(2)}) copy-start(s32[1024]{0:T(1024)S(1)} %get-tuple-element.1055) | copy-start | bytes 12292 | tf_op jit(solution)/shard_map/while
  8.6 99.5 %copy-start.41 = (pred[1024]{0:T(1024)(128)(4,1)}, pred[1024]{0:T(1024)(128)(4,1)S(1)}, u32[]{:S(2)}) copy-start(pred[1024]{0:T(1024)(128)(4,1)S(1)} %get-tuple-element.1056) | copy-start | bytes 3076 | tf_op jit(solution)/shard_map/while
  8.7 33.7 %copy-start.4 = (bf16[2,1,512,768]{3,2,1,0:T(8,128)(2,1)S(1)}, bf16[2,1,512,768]{3,2,1,0:T(8,128)(2,1)}, u32[]{:S(2)}) copy-start(bf16[2,1,512,768]{3,2,1,0:T(8,128)(2,1)} %get-tuple-element.1040) | copy-start | bytes 4718596 | tf_op jit(solution)/shard_map/while
  8.7 75.6 %all-gather.11.cloned.1.call-start = ((), (), s32[]{:S(2)}) async-start(), calls=%async_computation.10 | async-start | bytes 4423680 | tf_op jit(solution)/shard_map/while/body/eval_jaxpr/all_gather | solution.py:114
  9.4 146.5 %all-gather.9.cloned.1.call-start = ((), (), s32[]{:S(2)}) async-start(), calls=%async_computation.9 | async-start | bytes 1474560 | tf_op jit(solution)/shard_map/while/body/eval_jaxpr/all_gather | solution.py:117
  10.2 195.0 %all-gather.13.cloned.1.call-start = ((), (), s32[]{:S(2)}) async-start(), calls=%async_computation.11 | async-start | bytes 5898240 | tf_op jit(solution)/shard_map/while/body/eval_jaxpr/all_gather | solution.py:123
  10.9 283.6 %all-gather.15.cloned.1.call-start = ((), (), s32[]{:S(2)}) async-start(), calls=%async_computation.12 | async-start | bytes 5898240 | tf_op jit(solution)/shard_map/while/body/eval_jaxpr/all_gather | solution.py:163
  88.4 6.2 copy-start.40
  88.5 19.5 %copy-start.12 = (bf16[2,1,512,768]{3,2,1,0:T(8,128)(2,1)S(1)}, bf16[2,1,512,768]{3,2,1,0:T(8,128)(2,1)}, u32[]{:S(2)}) copy-start(bf16[2,1,512,768]{3,2,1,0:T(8,128)(2,1)} %get-tuple-element.1045) | copy-start | bytes 4718596 | tf_op jit(solution)/shard_map/while
  88.8 21.7 %collective-permute-start = (bf16[1,512,768]{2,1,0:T(8,128)(2,1)S(1)}, bf16[1,512,768]{2,1,0:T(8,128)(2,1)}, u32[]{:S(2)}, u32[]{:S(2)}) collective-permute-start(bf16[1,512,768]{2,1,0:T(8,128)(2,1)S(1)} %get-tuple-element.911), channel_id=1, source_target_pairs={{0,1},{2,3},{4,5},{6,7},{8,9},{10,11},{12,13},{14,15},{16,17},{18,... | collective-permute-start | bytes 2359304 | tf_op jit(solution)/shard_map/while/body/eval_jaxpr/ppermute | solution.py:14
  92.5 20.6 %collective-permute-start.1 = (bf16[1,512,768]{2,1,0:T(8,128)(2,1)}, bf16[1,512,768]{2,1,0:T(8,128)(2,1)}, u32[]{:S(2)}, u32[]{:S(2)}) collective-permute-start(bf16[1,512,768]{2,1,0:T(8,128)(2,1)} %slice.85), channel_id=1, source_target_pairs={{0,1},{2,3},{4,5},{6,7},{8,9},{10,11},{12,13},{14,15},{16,17},{18,... | collective-permute-start | bytes 2359304 | tf_op jit(solution)/shard_map/while/body/eval_jaxpr/ppermute | solution.py:14
  108.1 4.9 copy-start.23
  113.0 30.8 %copy-start = (bf16[1,1024,768]{1,2,0:T(8,128)(2,1)}, bf16[1,1024,768]{1,2,0:T(8,128)(2,1)S(1)}, u32[]{:S(2)}) copy-start(bf16[1,1024,768]{1,2,0:T(8,128)(2,1)S(1)} %copy.50) | copy-start | bytes 4718596 | tf_op jit(solution)/shard_map/while
  116.7 15.2 %copy-start.3 = (pred[512,1024]{1,0:T(8,128)(4,1)S(1)}, pred[512,1024]{1,0:T(8,128)(4,1)}, u32[]{:S(2)}) copy-start(pred[512,1024]{1,0:T(8,128)(4,1)} %fusion.200) | copy-start | bytes 1572868 | tf_op jit(solution)/shard_map/while
  158.9 135.6 %copy-start.13 = (bf16[2,1,512,768]{3,2,1,0:T(8,128)(2,1)S(1)}, bf16[2,1,512,768]{3,2,1,0:T(8,128)(2,1)}, u32[]{:S(2)}) copy-start(bf16[2,1,512,768]{3,2,1,0:T(8,128)(2,1)} %get-tuple-element.1045) | copy-start | bytes 4718596 | tf_op jit(solution)/shard_map/while
  294.5 9.3 copy-start.43
  312.2 13.6 %copy-start.1 = (bf16[1,1024,768]{1,2,0:T(8,128)(2,1)S(1)}, bf16[1,1024,768]{1,2,0:T(8,128)(2,1)}, u32[]{:S(2)}) copy-start(bf16[1,1024,768]{1,2,0:T(8,128)(2,1)} %copy-done) | copy-start | bytes 4718596 | tf_op jit(solution)/shard_map/while
  312.2 13.6 %copy-start.2 = (bf16[512,768]{0,1:T(8,128)(2,1)S(1)}, bf16[512,768]{0,1:T(8,128)(2,1)}, u32[]{:S(2)}) copy-start(bf16[512,768]{0,1:T(8,128)(2,1)} %copy.53) | copy-start | bytes 2359300 | tf_op jit(solution)/shard_map/while
  442.5 14.2 %copy-start.9 = (bf16[512,3072]{1,0:T(8,128)(2,1)S(1)}, bf16[512,3072]{1,0:T(8,128)(2,1)}, u32[]{:S(2)}) copy-start(bf16[512,3072]{1,0:T(8,128)(2,1)} %copy-done.8) | copy-start | bytes 9437188 | tf_op jit(solution)/shard_map/while
  455.4 20.5 %collective-permute-start.2 = (bf16[1,512,768]{1,2,0:T(8,128)(2,1)}, bf16[1,512,768]{1,2,0:T(8,128)(2,1)}, u32[]{:S(2)}, u32[]{:S(2)}) collective-permute-start(bf16[1,512,768]{1,2,0:T(8,128)(2,1)} %slice.86), channel_id=1, source_target_pairs={{1,0},{3,2},{5,4},{7,6},{9,8},{11,10},{13,12},{15,14},{17,16},{19,... | collective-permute-start | bytes 2359304 | tf_op jit(solution)/shard_map/while/body/eval_jaxpr/ppermute | solution.py:14
  463.9 14.9 %collective-permute-start.3 = (bf16[1,512,768]{1,2,0:T(8,128)(2,1)S(1)}, bf16[1,512,768]{1,2,0:T(8,128)(2,1)S(1)}, u32[]{:S(2)}, u32[]{:S(2)}) collective-permute-start(bf16[1,512,768]{1,2,0:T(8,128)(2,1)S(1)} %slice.87), channel_id=1, source_target_pairs={{1,0},{3,2},{5,4},{7,6},{9,8},{11,10},{13,12},{15,14},{17,16},{19,... | collective-permute-start | bytes 2359304 | tf_op jit(solution)/shard_map/while/body/eval_jaxpr/ppermute | solution.py:14
  465.2 9.2 copy-start.6
  465.2 9.2 copy-start.15
  478.8 7.9 copy-start.35
  479.5 7.3 copy-start.44
  492.0 96.5 %copy-start.21 = (s32[1024]{0:T(1024)}, s32[1024]{0:T(1024)S(1)}, u32[]{:S(2)}) copy-start(s32[1024]{0:T(1024)S(1)} %get-tuple-element.1055) | copy-start | bytes 12292 | tf_op jit(solution)/shard_map/while
  492.0 96.5 %copy-start.41 = (pred[1024]{0:T(1024)(128)(4,1)}, pred[1024]{0:T(1024)(128)(4,1)S(1)}, u32[]{:S(2)}) copy-start(pred[1024]{0:T(1024)(128)(4,1)S(1)} %get-tuple-element.1056) | copy-start | bytes 3076 | tf_op jit(solution)/shard_map/while
  492.0 28.5 %copy-start.4 = (bf16[2,1,512,768]{3,2,1,0:T(8,128)(2,1)S(1)}, bf16[2,1,512,768]{3,2,1,0:T(8,128)(2,1)}, u32[]{:S(2)}) copy-start(bf16[2,1,512,768]{3,2,1,0:T(8,128)(2,1)} %get-tuple-element.1040) | copy-start | bytes 4718596 | tf_op jit(solution)/shard_map/while
  492.1 72.5 %all-gather.11.cloned.1.call-start = ((), (), s32[]{:S(2)}) async-start(), calls=%async_computation.10 | async-start | bytes 4423680 | tf_op jit(solution)/shard_map/while/body/eval_jaxpr/all_gather | solution.py:114
  492.7 143.5 %all-gather.9.cloned.1.call-start = ((), (), s32[]{:S(2)}) async-start(), calls=%async_computation.9 | async-start | bytes 1474560 | tf_op jit(solution)/shard_map/while/body/eval_jaxpr/all_gather | solution.py:117
  493.2 192.3 %all-gather.13.cloned.1.call-start = ((), (), s32[]{:S(2)}) async-start(), calls=%async_computation.11 | async-start | bytes 5898240 | tf_op jit(solution)/shard_map/while/body/eval_jaxpr/all_gather | solution.py:123
  494.0 281.0 %all-gather.15.cloned.1.call-start = ((), (), s32[]{:S(2)}) async-start(), calls=%async_computation.12 | async-start | bytes 5898240 | tf_op jit(solution)/shard_map/while/body/eval_jaxpr/all_gather | solution.py:163
  568.8 6.3 copy-start.40
  568.8 19.6 %copy-start.12 = (bf16[2,1,512,768]{3,2,1,0:T(8,128)(2,1)S(1)}, bf16[2,1,512,768]{3,2,1,0:T(8,128)(2,1)}, u32[]{:S(2)}) copy-start(bf16[2,1,512,768]{3,2,1,0:T(8,128)(2,1)} %get-tuple-element.1045) | copy-start | bytes 4718596 | tf_op jit(solution)/shard_map/while
  569.1 21.8 %collective-permute-start = (bf16[1,512,768]{2,1,0:T(8,128)(2,1)S(1)}, bf16[1,512,768]{2,1,0:T(8,128)(2,1)}, u32[]{:S(2)}, u32[]{:S(2)}) collective-permute-start(bf16[1,512,768]{2,1,0:T(8,128)(2,1)S(1)} %get-tuple-element.911), channel_id=1, source_target_pairs={{0,1},{2,3},{4,5},{6,7},{8,9},{10,11},{12,13},{14,15},{16,17},{18,... | collective-permute-start | bytes 2359304 | tf_op jit(solution)/shard_map/while/body/eval_jaxpr/ppermute | solution.py:14
  572.9 20.3 %collective-permute-start.1 = (bf16[1,512,768]{2,1,0:T(8,128)(2,1)}, bf16[1,512,768]{2,1,0:T(8,128)(2,1)}, u32[]{:S(2)}, u32[]{:S(2)}) collective-permute-start(bf16[1,512,768]{2,1,0:T(8,128)(2,1)} %slice.85), channel_id=1, source_target_pairs={{0,1},{2,3},{4,5},{6,7},{8,9},{10,11},{12,13},{14,15},{16,17},{18,... | collective-permute-start | bytes 2359304 | tf_op jit(solution)/shard_map/while/body/eval_jaxpr/ppermute | solution.py:14
  588.5 4.7 copy-start.23
  593.2 30.8 %copy-start = (bf16[1,1024,768]{1,2,0:T(8,128)(2,1)}, bf16[1,1024,768]{1,2,0:T(8,128)(2,1)S(1)}, u32[]{:S(2)}) copy-start(bf16[1,1024,768]{1,2,0:T(8,128)(2,1)S(1)} %copy.50) | copy-start | bytes 4718596 | tf_op jit(solution)/shard_map/while
  596.9 15.3 %copy-start.3 = (pred[512,1024]{1,0:T(8,128)(4,1)S(1)}, pred[512,1024]{1,0:T(8,128)(4,1)}, u32[]{:S(2)}) copy-start(pred[512,1024]{1,0:T(8,128)(4,1)} %fusion.200) | copy-start | bytes 1572868 | tf_op jit(solution)/shard_map/while
  639.1 135.9 %copy-start.13 = (bf16[2,1,512,768]{3,2,1,0:T(8,128)(2,1)S(1)}, bf16[2,1,512,768]{3,2,1,0:T(8,128)(2,1)}, u32[]{:S(2)}) copy-start(bf16[2,1,512,768]{3,2,1,0:T(8,128)(2,1)} %get-tuple-element.1045) | copy-start | bytes 4718596 | tf_op jit(solution)/shard_map/while
  775.0 9.7 copy-start.43
  793.1 13.6 %copy-start.1 = (bf16[1,1024,768]{1,2,0:T(8,128)(2,1)S(1)}, bf16[1,1024,768]{1,2,0:T(8,128)(2,1)}, u32[]{:S(2)}) copy-start(bf16[1,1024,768]{1,2,0:T(8,128)(2,1)} %copy-done) | copy-start | bytes 4718596 | tf_op jit(solution)/shard_map/while
  793.1 13.6 %copy-start.2 = (bf16[512,768]{0,1:T(8,128)(2,1)S(1)}, bf16[512,768]{0,1:T(8,128)(2,1)}, u32[]{:S(2)}) copy-start(bf16[512,768]{0,1:T(8,128)(2,1)} %copy.53) | copy-start | bytes 2359300 | tf_op jit(solution)/shard_map/while
  923.2 16.9 %copy-start.9 = (bf16[512,3072]{1,0:T(8,128)(2,1)S(1)}, bf16[512,3072]{1,0:T(8,128)(2,1)}, u32[]{:S(2)}) copy-start(bf16[512,3072]{1,0:T(8,128)(2,1)} %copy-done.8) | copy-start | bytes 9437188 | tf_op jit(solution)/shard_map/while
  938.8 22.8 %collective-permute-start.2 = (bf16[1,512,768]{1,2,0:T(8,128)(2,1)}, bf16[1,512,768]{1,2,0:T(8,128)(2,1)}, u32[]{:S(2)}, u32[]{:S(2)}) collective-permute-start(bf16[1,512,768]{1,2,0:T(8,128)(2,1)} %slice.86), channel_id=1, source_target_pairs={{1,0},{3,2},{5,4},{7,6},{9,8},{11,10},{13,12},{15,14},{17,16},{19,... | collective-permute-start | bytes 2359304 | tf_op jit(solution)/shard_map/while/body/eval_jaxpr/ppermute | solution.py:14
  949.6 15.0 %collective-permute-start.3 = (bf16[1,512,768]{1,2,0:T(8,128)(2,1)S(1)}, bf16[1,512,768]{1,2,0:T(8,128)(2,1)S(1)}, u32[]{:S(2)}, u32[]{:S(2)}) collective-permute-start(bf16[1,512,768]{1,2,0:T(8,128)(2,1)S(1)} %slice.87), channel_id=1, source_target_pairs={{1,0},{3,2},{5,4},{7,6},{9,8},{11,10},{13,12},{15,14},{17,16},{19,... | collective-permute-start | bytes 2359304 | tf_op jit(solution)/shard_map/while/body/eval_jaxpr/ppermute | solution.py:14
  950.9 9.2 copy-start.6
  950.9 9.2 copy-start.15
  964.5 10.1 copy-start.35
  965.1 9.5 copy-start.44
  983.0 32.7 %reduce-scatter.7.cloned.1.call-start = ((), (), s32[]{:S(2)}) async-start(), calls=%async_computation.5 | async-start | bytes 1474560 | tf_op jit(solution)/shard_map/reduce_scatter | solution.py:231
  985.9 97.0 %reduce-scatter.5.cloned.1.call-start = ((), (), s32[]{:S(2)}) async-start(), calls=%async_computation.4 | async-start | bytes 4423680 | tf_op jit(solution)/shard_map/reduce_scatter | solution.py:231
  991.1 179.3 %reduce-scatter.9.cloned.1.call-start = ((), (), s32[]{:S(2)}) async-start(), calls=%async_computation.6 | async-start | bytes 5898240 | tf_op jit(solution)/shard_map/reduce_scatter | solution.py:231
  998.0 260.5 %reduce-scatter.11.cloned.1.call-start = ((), (), s32[]{:S(2)}) async-start(), calls=%async_computation.7 | async-start | bytes 5898240 | tf_op jit(solution)/shard_map/reduce_scatter | solution.py:231
  1004.4 254.1 %copy-start.49 = (u32[32]{0:T(128)S(1)}, u32[32]{0:T(128)}, u32[]{:S(2)}) copy-start(u32[32]{0:T(128)} %get-tuple-element.1116) | copy-start | bytes 388
  1004.4 256.0 %copy-start.39 = (f32[768]{0:T(1024)S(1)}, f32[768]{0:T(1024)}, u32[]{:S(2)}) copy-start(f32[768]{0:T(1024)} %get-tuple-element.421) | copy-start | bytes 9220
  1004.4 256.0 %copy-start.36 = (f32[768]{0:T(1024)S(1)}, f32[768]{0:T(1024)}, u32[]{:S(2)}) copy-start(f32[768]{0:T(1024)} %get-tuple-element.422) | copy-start | bytes 9220
  1004.4 256.0 %copy-start.33 = (f32[768]{0:T(1024)S(1)}, f32[768]{0:T(1024)}, u32[]{:S(2)}) copy-start(f32[768]{0:T(1024)} %get-tuple-element.424) | copy-start | bytes 9220
  1004.4 256.0 %copy-start.30 = (f32[768]{0:T(1024)S(1)}, f32[768]{0:T(1024)}, u32[]{:S(2)}) copy-start(f32[768]{0:T(1024)} %get-tuple-element.425) | copy-start | bytes 9220
  1004.4 256.1 %copy-start.27 = (f32[768]{0:T(1024)S(1)}, f32[768]{0:T(1024)}, u32[]{:S(2)}) copy-start(f32[768]{0:T(1024)} %get-tuple-element.426) | copy-start | bytes 9220
  1004.4 256.1 %copy-start.20 = (f32[3072]{0:T(1024)S(1)}, f32[3072]{0:T(1024)}, u32[]{:S(2)}) copy-start(f32[3072]{0:T(1024)} %get-tuple-element.430) | copy-start | bytes 36868
  1004.5 332.5 %all-reduce.33.cloned.1.call-start = ((), (), s32[]{:S(2)}) async-start(), calls=%async_computation.8 | async-start | bytes 7077888 | tf_op jit(solution)/shard_map/psum | solution.py:234
  1336.9 4.5 copy-start.17
  1338.8 4.3 copy-start.16
  (48 other events, 117.0 us)
Sparse Core Ops, SparseCore 0:
  11.1 73.1 all-gather.10
  85.9 29.1 all-gather.8
  116.6 88.5 all-gather.12
  206.6 87.8 all-gather.14
  494.2 70.3 all-gather.10
  566.0 29.3 all-gather.8
  597.0 88.5 all-gather.12
  687.1 87.8 all-gather.14
Sparse Core Ops, SparseCore 1:
  986.4 29.2 reduce-scatter.6
  1017.9 65.0 reduce-scatter.4
  1085.1 85.3 reduce-scatter.8
  1172.8 85.6 reduce-scatter.10
  1262.2 74.7 all-reduce.32
where the time goes:
time: 1360 us; the launch traced here: 1350 us
  waiting for transfers between devices  640 us (47%)
  matrix products  452 us (33%)
  blocking collectives  94.9 us (7%)
  other arithmetic  79.7 us (6%)
  local copies, waits for them, and re-layouts  45.7 us (3%)
  between operations  17.5 us (1%)
  starting transfers between devices  15.6 us (1%)
    reduce_scatter x4, waiting for transfers between devices, local(): lax.psum_scatter(for_sending(totals), 'fsdp', scatter_dimension=0, tiled=...  254 us
    all_gather x2, waiting for transfers between devices, micro(): lax.all_gather(shards[11], 'fsdp', axis=0, tiled=True)  165 us
    dot_general x2, matrix products, micro(): jnp.einsum('shqk,sqhd->skhd', d_scores, query_heads, preferred_element_ty...  108 us
    dot_general x2, matrix products, micro(): jnp.einsum('shqk,skhd->sqhd', d_scores, key_heads, preferred_element_type...  105 us
    all_gather x2, waiting for transfers between devices, micro(): lax.all_gather(shards[9], 'fsdp', axis=0, tiled=True)  92.7 us
    all_gather x2, waiting for transfers between devices, micro(): lax.all_gather(shards[0], 'fsdp', axis=0, tiled=True)  85.2 us
    dot_general x8, matrix products, outer_sum(): jnp.einsum('sri,srj->ij', left, right, preferred_element_type=jnp.float32)  56.7 us
    dot_general x8, matrix products, project(): jnp.einsum('sri,ij->srj', left, weight, preferred_element_type=jnp.float32)  46.1 us
  transfers between devices with their start and end apart: 21, of which 11 were waited for; matrix products, arithmetic and copies ran while one was open for 16% of the time, Pallas kernels for 0%

commit v1 on v0

--- a/solution.py
+++ b/solution.py
@@ -6,6 +6,27 @@
 
 H = 12
 EPS = 1e-05
+
+
+def collect(array, axis, dim):
+    size, index, width = (lax.axis_size(axis), lax.axis_index(axis), array.shape[dim])
+    upward = [(i, (i + 1) % size) for i in range(size)]
+    left = [(i, (i - 1) % size) for i in range(size)]
+    out = jnp.zeros((*array.shape[:dim], size * width, *array.shape[dim + 1 :]), array.dtype)
+    out = lax.dynamic_update_slice_in_dim(out, array, index * width, axis=dim)
+    from_left = from_right = array
+    half = size // 2
+    for step in range(1, half + 1):
+        from_left = lax.ppermute(from_left, axis, upward)
+        out = lax.dynamic_update_slice_in_dim(
+            out, from_left, (index - step) % size * width, axis=dim
+        )
+        if step < size - half:
+            from_right = lax.ppermute(from_right, axis, left)
+            out = lax.dynamic_update_slice_in_dim(
+                out, from_right, (index + step) % size * width, axis=dim
+            )
+    return out
 
 
 def from_behind(x, axis, by):
@@ -160,7 +181,7 @@
             lax.all_gather(shards[8], "fsdp", axis=0, tiled=True),
             lax.all_gather(shards[9], "fsdp", axis=0, tiled=True),
             lax.all_gather(shards[10], "fsdp", axis=0, tiled=True),
-            lax.all_gather(shards[11], "fsdp", axis=0, tiled=True),
+            collect(shards[11], "fsdp", 0),
             lax.all_gather(shards[12], "fsdp", axis=0, tiled=True),
         )
         grad_out = grad_in.astype(f32)

time: 1360 us -> 1270 us (0.934)
  waiting for transfers between devices: 640 us -> 541 us
  local copies, waits for them, and re-layouts: 45.7 us -> 65.3 us
    all_gather x2, waiting for transfers between devices: 165 us -> 0.01 us  [micro(): lax.all_gather(shards[11], 'fsdp', axis=0, tiled=True)]
    ppermute x0 -> x3, waiting for transfers between devices: none -> 76.7 us  [the longest x2 52.8 us: collect(): from_left = lax.ppermute(from_left, axis, upward)]
    all_gather x2, waiting for transfers between devices: 92.7 us -> 72.9 us  [micro(): lax.all_gather(shards[9], 'fsdp', axis=0, tiled=True)]
    dynamic_update_slice x0 -> x8, local copies, waits for them, and re-layouts: none -> 16.7 us  [the longest x4 9.73 us: collect(): lax.dynamic_update_slice_in_dim(out, from_left, (index - step) % size * w...]
  transfers between devices with their start and end apart: 21 -> 24, of which waited for: 11 -> 12; matrix products, arithmetic and copies ran while one was open for 16% -> 43% of each run, Pallas kernels for 0% -> 0%
where the time goes in v1:
time: 1270 us
  waiting for transfers between devices  541 us (43%)
  matrix products  448 us (35%)
  blocking collectives  90.5 us (7%)
  other arithmetic  80.2 us (6%)
  local copies, waits for them, and re-layouts  65.3 us (5%)
  starting transfers between devices  20.5 us (2%)
  between operations  17.5 us (1%)
    reduce_scatter x4, waiting for transfers between devices, local(): lax.psum_scatter(for_sending(totals), 'fsdp', scatter_dimension=0, tiled=...  254 us
    dot_general x2, matrix products, micro(): jnp.einsum('shqk,sqhd->skhd', d_scores, query_heads, preferred_element_ty...  108 us
    dot_general x2, matrix products, micro(): jnp.einsum('shqk,skhd->sqhd', d_scores, key_heads, preferred_element_type...  105 us
    all_gather x2, waiting for transfers between devices, micro(): lax.all_gather(shards[0], 'fsdp', axis=0, tiled=True)  91.2 us
    all_gather x2, waiting for transfers between devices, micro(): lax.all_gather(shards[9], 'fsdp', axis=0, tiled=True)  72.9 us
    dot_general x8, matrix products, outer_sum(): jnp.einsum('sri,srj->ij', left, right, preferred_element_type=jnp.float32)  59.6 us
    ppermute x2, waiting for transfers between devices, collect(): from_left = lax.ppermute(from_left, axis, upward)  52.8 us
    dot_general x8, matrix products, project(): jnp.einsum('sri,ij->srj', left, weight, preferred_element_type=jnp.float32)  41.5 us
  transfers between devices with their start and end apart: 24, of which 12 were waited for; matrix products, arithmetic and copies ran while one was open for 43% of the time, Pallas kernels for 0%

profile of v1, /device:TPU:0, one launch (start us, length us, event | category | flops | bytes accessed | tf_op | source)
XLA Modules:
  0.0 1268.6 jit_solution(4901477788543122277)
XLA Ops:
  8.0 3.1 collective-permute-start.4
  13.2 27.1 %collective-permute-done.4 = bf16[768,768]{1,0:T(8,128)(2,1)} collective-permute-done((bf16[768,768]{1,0:T(8,128)(2,1)}, bf16[768,768]{1,0:T(8,128)(2,1)}, u32[]{:S(2)}, u32[]{:S(2)}) %collective-permute-start.4) | collective-permute-done | bytes 1179680 | tf_op jit(solution)/shard_map/while/body/eval_jaxpr/ppermute | solution.py:20
  40.4 23.9 %collective-permute-done.5 = bf16[768,768]{1,0:T(8,128)(2,1)} collective-permute-done((bf16[768,768]{1,0:T(8,128)(2,1)}, bf16[768,768]{1,0:T(8,128)(2,1)}, u32[]{:S(2)}, u32[]{:S(2)}) %collective-permute-start.5) | collective-permute-done | bytes 1179680 | tf_op jit(solution)/shard_map/while/body/eval_jaxpr/ppermute | solution.py:25
  64.3 25.7 %collective-permute-done.6 = bf16[768,768]{1,0:T(8,128)(2,1)} collective-permute-done((bf16[768,768]{1,0:T(8,128)(2,1)}, bf16[768,768]{1,0:T(8,128)(2,1)}, u32[]{:S(2)}, u32[]{:S(2)}) %collective-permute-start.6) | collective-permute-done | bytes 1179680 | tf_op jit(solution)/shard_map/while/body/eval_jaxpr/ppermute | solution.py:20
  90.0 808.5 %while.41 = (s32[]{:T(128)}, f32[768,2304]{1,0:T(8,128)}, f32[768]{0:T(1024)}, f32[768]{0:T(1024)}, f32[768,768]{1,0:T(8,128)}, /*index=5*/f32[768]{0:T(1024)}, ...) while((s32[]{:T(128)}, f32[768,2304]{1,0:T(8,128)}, ...), condition=%wide.region_21.22_spmd.clone, body=%wide.region_0.21_spmd.clone.sunk | while | flops 26950144000 | bytes 763714880 | solution.py:249
  96.7 17.7 %all-reduce.30 = (bf16[768]{0:T(1024)(128)(2,1)S(1)}, bf16[768]{0:T(1024)(128)(2,1)S(1)}, bf16[768]{0:T(1024)(128)(2,1)S(1)}, bf16[768]{0:T(1024)(128)(2,1)S(1)}...) all-reduce(bf16[768]{0:T(1024)(128)(2,1)S(1)} %dynamic-update-slice, ...), channel_id=1, replica_groups=mesh['rep'=4,'fsdp'=4,'ctx'=2] {'fsdp'}, use_global_device_ids=true, to_apply=%add.1 | all-reduce | flops 6144 | bytes 24576 | tf_op jit(solution)/shard_map/while
  117.9 44.2 %all-gather.11.cloned.1.call-done = bf16[768,2304]{1,0:T(8,128)(2,1)} async-done(((bf16[192,2304]{1,0:T(8,128)(2,1)}), bf16[768,2304]{1,0:T(8,128)(2,1)}) %all-gather.11.cloned.1.call-update) | async-done | bytes 3538960 | tf_op jit(solution)/shard_map/while/body/eval_jaxpr/all_gather | solution.py:135
  162.1 4.2 convolution_bitcast_fusion.2
  168.8 2.6 collective-permute-start
  171.5 2.5 constant_dynamic-update-slice_fusion.9
  180.9 13.1 %all-gather.3 = bf16[4,1,768]{2,1,0:T(2,128)(2,1)S(1)} all-gather(bf16[1,1,768]{2,1,0:T(2,128)(2,1)S(1)} %reshape.647), channel_id=1, replica_groups=mesh['rep'=4,'fsdp'=4,'ctx'=2] {'fsdp'}, dimensions={0}, use_global_device_ids=true | all-gather | bytes 7680 | tf_op jit(solution)/shard_map/while/body/eval_jaxpr/all_gather | solution.py:145
  205.2 14.5 %fusion.201 = (f32[12,512]{1,0:T(8,128)S(1)}, f32[12,512,1024]{2,1,0:T(8,128)}) fusion(pred[512,1024]{1,0:T(8,128)(4,1)} %fusion.200, bf16[512,12,64]{0,2,1:T(8,128)(2,1)} %bitcast.212, bf16[1024,12,64]{0,2,1:T(8,128)(2,1)} %bitcast.210), kind=kOutput, calls=%fused_computation.8.clone.1 | convolution fusion | flops 824174592 | bytes 28073984 | tf_op jit(solution)/shard_map/while/body/eval_jaxpr/sqhd,skhd->shqk/dot_general | solution.py:82
  219.7 11.9 exponential_reduce_fusion.2
  231.6 12.0 convolution_convert_fusion.4
  243.6 2.6 fusion.202
  246.6 36.4 %all-gather.13.cloned.1.call-done = bf16[768,3072]{1,0:T(8,128)(2,1)} async-done(((bf16[192,3072]{1,0:T(8,128)(2,1)}), bf16[768,3072]{1,0:T(8,128)(2,1)}) %all-gather.13.cloned.1.call-update) | async-done | bytes 4718608 | tf_op jit(solution)/shard_map/while/body/eval_jaxpr/all_gather | solution.py:144
  283.1 4.8 fusion.203
  287.9 10.5 convert_reduce_fusion.13
  298.5 3.0 multiply_reduce_fusion.9
  306.9 12.0 fusion.204
  322.9 10.3 fusion.205
  333.2 52.3 %convert_reduce_fusion.16 = (f32[12,64]{1,0:T(8,128)S(1)}, bf16[12,64,512]{2,1,0:T(8,128)(2,1)}) fusion(bf16[1024,12,64]{0,2,1:T(8,128)(2,1)} %bitcast.211, f32[12,512,1024]{2,1,0:T(8,128)} %fusion.205, f32[12,512]{1,0:T(8,128)S(1)} %log_add_fusion.2, f32[12,512,1024]{2,1,0:T(8,128)} %get-tuple-element.967, pred[512,1024]{1,0:T(8,128)(4,1)} %fusion.200), kind=kOutput, calls=%fused_computation.77.clone.1 | convolution fusion | flops 875698432 | bytes 53242880 | tf_op jit(solution)/shard_map/while/body/eval_jaxpr/shqk,skhd->sqhd/dot_general | solution.py:211
  385.6 54.1 %fusion.206 = f32[12,64,1024]{2,1,0:T(8,128)} fusion(bf16[512,12,64]{0,2,1:T(8,128)(2,1)} %bitcast.213, f32[12,512,1024]{2,1,0:T(8,128)} %fusion.205, f32[12,512]{1,0:T(8,128)S(1)} %log_add_fusion.2, f32[12,512,1024]{2,1,0:T(8,128)} %get-tuple-element.967, pred[512,1024]{1,0:T(8,128)(4,1)} %fusion.200), kind=kOutput, calls=%fused_computation.10.clone.1 | convolution fusion | flops 874519552 | bytes 54812672 | tf_op jit(solution)/shard_map/while/body/eval_jaxpr/shqk,sqhd->skhd/dot_general | solution.py:213
  443.4 7.6 select_add_fusion.29
  451.0 10.1 select_add_fusion.31
  461.2 9.1 fusion.209
  472.2 2.5 convert_reduce_fusion.15
  476.3 7.6 select_add_fusion.23
  483.9 2.7 fusion.208
  495.7 16.1 %all-reduce.30 = (bf16[768]{0:T(1024)(128)(2,1)S(1)}, bf16[768]{0:T(1024)(128)(2,1)S(1)}, bf16[768]{0:T(1024)(128)(2,1)S(1)}, bf16[768]{0:T(1024)(128)(2,1)S(1)}...) all-reduce(bf16[768]{0:T(1024)(128)(2,1)S(1)} %dynamic-update-slice, ...), channel_id=1, replica_groups=mesh['rep'=4,'fsdp'=4,'ctx'=2] {'fsdp'}, use_global_device_ids=true, to_apply=%add.1 | all-reduce | flops 6144 | bytes 24576 | tf_op jit(solution)/shard_map/while
  515.3 47.0 %all-gather.11.cloned.1.call-done = bf16[768,2304]{1,0:T(8,128)(2,1)} async-done(((bf16[192,2304]{1,0:T(8,128)(2,1)}), bf16[768,2304]{1,0:T(8,128)(2,1)}) %all-gather.11.cloned.1.call-update) | async-done | bytes 3538960 | tf_op jit(solution)/shard_map/while/body/eval_jaxpr/all_gather | solution.py:135
  562.4 4.2 convolution_bitcast_fusion.2
  569.1 2.7 collective-permute-start
  581.2 13.1 %all-gather.3 = bf16[4,1,768]{2,1,0:T(2,128)(2,1)S(1)} all-gather(bf16[1,1,768]{2,1,0:T(2,128)(2,1)S(1)} %reshape.647), channel_id=1, replica_groups=mesh['rep'=4,'fsdp'=4,'ctx'=2] {'fsdp'}, dimensions={0}, use_global_device_ids=true | all-gather | bytes 7680 | tf_op jit(solution)/shard_map/while/body/eval_jaxpr/all_gather | solution.py:145
  605.4 14.5 %fusion.201 = (f32[12,512]{1,0:T(8,128)S(1)}, f32[12,512,1024]{2,1,0:T(8,128)}) fusion(pred[512,1024]{1,0:T(8,128)(4,1)} %fusion.200, bf16[512,12,64]{0,2,1:T(8,128)(2,1)} %bitcast.212, bf16[1024,12,64]{0,2,1:T(8,128)(2,1)} %bitcast.210), kind=kOutput, calls=%fused_computation.8.clone.1 | convolution fusion | flops 824174592 | bytes 28073984 | tf_op jit(solution)/shard_map/while/body/eval_jaxpr/sqhd,skhd->shqk/dot_general | solution.py:82
  619.9 11.9 exponential_reduce_fusion.2
  631.8 12.0 convolution_convert_fusion.4
  643.8 2.6 fusion.202
  646.8 36.4 %all-gather.13.cloned.1.call-done = bf16[768,3072]{1,0:T(8,128)(2,1)} async-done(((bf16[192,3072]{1,0:T(8,128)(2,1)}), bf16[768,3072]{1,0:T(8,128)(2,1)}) %all-gather.13.cloned.1.call-update) | async-done | bytes 4718608 | tf_op jit(solution)/shard_map/while/body/eval_jaxpr/all_gather | solution.py:144
  683.2 4.8 fusion.203
  688.1 10.5 convert_reduce_fusion.13
  698.7 3.0 multiply_reduce_fusion.9
  707.0 12.0 fusion.204
  723.0 10.3 fusion.205
  733.3 52.3 %convert_reduce_fusion.16 = (f32[12,64]{1,0:T(8,128)S(1)}, bf16[12,64,512]{2,1,0:T(8,128)(2,1)}) fusion(bf16[1024,12,64]{0,2,1:T(8,128)(2,1)} %bitcast.211, f32[12,512,1024]{2,1,0:T(8,128)} %fusion.205, f32[12,512]{1,0:T(8,128)S(1)} %log_add_fusion.2, f32[12,512,1024]{2,1,0:T(8,128)} %get-tuple-element.967, pred[512,1024]{1,0:T(8,128)(4,1)} %fusion.200), kind=kOutput, calls=%fused_computation.77.clone.1 | convolution fusion | flops 875698432 | bytes 53242880 | tf_op jit(solution)/shard_map/while/body/eval_jaxpr/shqk,skhd->sqhd/dot_general | solution.py:211
  785.7 54.1 %fusion.206 = f32[12,64,1024]{2,1,0:T(8,128)} fusion(bf16[512,12,64]{0,2,1:T(8,128)(2,1)} %bitcast.213, f32[12,512,1024]{2,1,0:T(8,128)} %fusion.205, f32[12,512]{1,0:T(8,128)S(1)} %log_add_fusion.2, f32[12,512,1024]{2,1,0:T(8,128)} %get-tuple-element.967, pred[512,1024]{1,0:T(8,128)(4,1)} %fusion.200), kind=kOutput, calls=%fused_computation.10.clone.1 | convolution fusion | flops 874519552 | bytes 54812672 | tf_op jit(solution)/shard_map/while/body/eval_jaxpr/shqk,sqhd->skhd/dot_general | solution.py:213
  843.6 9.0 select_add_fusion.29
  852.6 12.9 %select_add_fusion.31 = f32[3072,768]{1,0:T(8,128)} fusion(f32[3072,768]{1,0:T(8,128)} %get-tuple-element.1061, pred[]{:T(512)S(6)} %compare.6, bf16[2,1,512,768]{3,2,1,0:T(8,128)(2,1)S(1)} %copy-done.17, s32[]{:T(128)S(6)} %copy.84, f32[512,3072]{1,0:T(8,128)} %copy-done.61, f32[3072]{0:T(1024)S(1)} %bitcast.221), kind=kOutput, calls=%fused_computation.12.clone.1 | convolution fusion | flops 2436366336 | bytes 25964548 | tf_op jit(solution)/shard_map/while/body/eval_jaxpr/sri,srj->ij/dot_general | solution.py:66
  865.4 9.1 fusion.209
  876.5 2.5 convert_reduce_fusion.15
  880.6 9.8 select_add_fusion.23
  890.4 2.7 fusion.208
  898.6 2.8 convert_element_type.440
  901.4 5.2 convert_element_type.434
  906.8 6.8 convert_element_type.452
  913.6 6.4 convert_element_type.456
  920.1 11.7 reduce-scatter.7.cloned.1.call-done
  931.8 67.2 %reduce-scatter.5.cloned.1.call-done = bf16[192,2304]{1,0:T(8,128)(2,1)} async-done(((bf16[768,2304]{1,0:T(8,128)(2,1)}), bf16[192,2304]{1,0:T(8,128)(2,1)}) %reduce-scatter.5.cloned.1.call-update) | async-done | bytes 884752 | tf_op jit(solution)/shard_map/reduce_scatter | solution.py:252
  999.0 87.5 %reduce-scatter.9.cloned.1.call-done = bf16[192,3072]{1,0:T(8,128)(2,1)} async-done(((bf16[768,3072]{1,0:T(8,128)(2,1)}), bf16[192,3072]{1,0:T(8,128)(2,1)}) %reduce-scatter.9.cloned.1.call-update) | async-done | bytes 1179664 | tf_op jit(solution)/shard_map/reduce_scatter | solution.py:252
  1086.5 88.0 %reduce-scatter.11.cloned.1.call-done = bf16[768,768]{1,0:T(8,128)(2,1)} async-done(((bf16[3072,768]{1,0:T(8,128)(2,1)}), bf16[768,768]{1,0:T(8,128)(2,1)}) %reduce-scatter.11.cloned.1.call-update) | async-done | bytes 1179664 | tf_op jit(solution)/shard_map/reduce_scatter | solution.py:252
  1176.7 18.3 %all-reduce.28 = (bf16[768]{0:T(1024)(128)(2,1)S(1)}, bf16[768]{0:T(1024)(128)(2,1)S(1)}, bf16[768]{0:T(1024)(128)(2,1)S(1)}, bf16[768]{0:T(1024)(128)(2,1)S(1)}...) all-reduce(bf16[768]{0:T(1024)(128)(2,1)S(1)} %convert_element_type, ...), channel_id=3, replica_groups=mesh['rep'=4,'fsdp'=4,'ctx'=2] {'fsdp'}, use_global_device_ids=true, to_apply=%region_24.25.clone | all-reduce | flops 9216 | bytes 36864
  1195.6 12.1 all-reduce.26
  1212.9 40.2 %all-reduce.33.cloned.1.call-done = (bf16[192,2304]{1,0:T(8,128)(2,1)}, bf16[192,768]{1,0:T(8,128)(2,1)}, bf16[192,3072]{1,0:T(8,128)(2,1)}, bf16[768,768]{1,0:T(8,128)(2,1)}) async-done(((bf16[192,2304]{1,0:T(8,128)(2,1)}, bf16[192,768]{1,0:T(8,128)(2,1)}, bf16[192,3072]{1,0:T(8,128)(2,1)}, bf16[768,768]{1,0:T(8,128)(2,1)}), (bf16[192,2304]{1,0:T(8,128)(2,1)}, bf16[192,768]{1,0:T(8,128)(2,1)}, ...) | async-done | bytes 3538960 | tf_op jit(solution)/shard_map/psum | solution.py:255
  1255.0 2.6 convert_element_type.435
  (467 shorter events, 113.8 us)
Async XLA Ops:
  8.0 32.3 %collective-permute-start.4 = (bf16[768,768]{1,0:T(8,128)(2,1)}, bf16[768,768]{1,0:T(8,128)(2,1)}, u32[]{:S(2)}, u32[]{:S(2)}) collective-permute-start(bf16[768,768]{1,0:T(8,128)(2,1)} %param.29), channel_id=1, source_target_pairs={{0,2},{2,4},{4,6},{6,0},{1,3},{3,5},{5,7},{7,1},{8,10},{10,12},{12... | collective-permute-start | bytes 3538952 | tf_op jit(solution)/shard_map/while/body/eval_jaxpr/ppermute | solution.py:20
  11.1 53.2 %collective-permute-start.5 = (bf16[768,768]{1,0:T(8,128)(2,1)}, bf16[768,768]{1,0:T(8,128)(2,1)}, u32[]{:S(2)}, u32[]{:S(2)}) collective-permute-start(bf16[768,768]{1,0:T(8,128)(2,1)} %param.29), channel_id=1, source_target_pairs={{0,6},{2,0},{4,2},{6,4},{1,7},{3,1},{5,3},{7,5},{8,14},{10,8},{12,... | collective-permute-start | bytes 3538952 | tf_op jit(solution)/shard_map/while/body/eval_jaxpr/ppermute | solution.py:25
  40.3 49.7 %collective-permute-start.6 = (bf16[768,768]{1,0:T(8,128)(2,1)}, bf16[768,768]{1,0:T(8,128)(2,1)}, u32[]{:S(2)}, u32[]{:S(2)}) collective-permute-start(bf16[768,768]{1,0:T(8,128)(2,1)} %collective-permute-done.4), channel_id=1, source_target_pairs={{0,2},{2,4},{4,6},{6,0},{1,3},{3,5},{5,7},{7,1},{8,10},{10,12},{12... | collective-permute-start | bytes 3538952 | tf_op jit(solution)/shard_map/while/body/eval_jaxpr/ppermute | solution.py:20
  90.0 106.7 %copy-start.24 = (s32[1024]{0:T(1024)}, s32[1024]{0:T(1024)S(1)}, u32[]{:S(2)}) copy-start(s32[1024]{0:T(1024)S(1)} %get-tuple-element.1133) | copy-start | bytes 12292 | tf_op jit(solution)/shard_map/while
  90.0 106.7 %copy-start.44 = (pred[1024]{0:T(1024)(128)(4,1)}, pred[1024]{0:T(1024)(128)(4,1)S(1)}, u32[]{:S(2)}) copy-start(pred[1024]{0:T(1024)(128)(4,1)S(1)} %get-tuple-element.1134) | copy-start | bytes 3076 | tf_op jit(solution)/shard_map/while
  90.1 72.0 %all-gather.11.cloned.1.call-start = ((), (), s32[]{:S(2)}) async-start(), calls=%async_computation.10 | async-start | bytes 4423680 | tf_op jit(solution)/shard_map/while/body/eval_jaxpr/all_gather | solution.py:135
  90.9 152.8 %all-gather.9.cloned.1.call-start = ((), (), s32[]{:S(2)}) async-start(), calls=%async_computation.9 | async-start | bytes 1474560 | tf_op jit(solution)/shard_map/while/body/eval_jaxpr/all_gather | solution.py:138
  91.6 191.4 %all-gather.13.cloned.1.call-start = ((), (), s32[]{:S(2)}) async-start(), calls=%async_computation.11 | async-start | bytes 5898240 | tf_op jit(solution)/shard_map/while/body/eval_jaxpr/all_gather | solution.py:144
  92.3 368.8 %all-gather.15.cloned.1.call-start = ((), (), s32[]{:S(2)}) async-start(), calls=%async_computation.12 | async-start | bytes 5898240 | tf_op jit(solution)/shard_map/while/body/eval_jaxpr/all_gather | solution.py:146
  93.0 23.8 %copy-start.4 = (bf16[768,768]{1,0:T(8,128)(2,1)S(1)}, bf16[768,768]{1,0:T(8,128)(2,1)}, u32[]{:S(2)}) copy-start(bf16[768,768]{1,0:T(8,128)(2,1)} %get-tuple-element.1124) | copy-start | bytes 3538948 | tf_op jit(solution)/shard_map/while
  168.8 30.2 %collective-permute-start = (bf16[1,512,768]{2,1,0:T(8,128)(2,1)S(1)}, bf16[1,512,768]{2,1,0:T(8,128)(2,1)}, u32[]{:S(2)}, u32[]{:S(2)}) collective-permute-start(bf16[1,512,768]{2,1,0:T(8,128)(2,1)S(1)} %get-tuple-element.964), channel_id=1, source_target_pairs={{0,1},{2,3},{4,5},{6,7},{8,9},{10,11},{12,13},{14,15},{16,17},{18,... | collective-permute-start | bytes 2359304 | tf_op jit(solution)/shard_map/while/body/eval_jaxpr/ppermute | solution.py:35
  171.5 9.4 copy-start.43
  171.5 22.6 %copy-start.14 = (bf16[2,1,512,768]{3,2,1,0:T(8,128)(2,1)S(1)}, bf16[2,1,512,768]{3,2,1,0:T(8,128)(2,1)}, u32[]{:S(2)}) copy-start(bf16[2,1,512,768]{3,2,1,0:T(8,128)(2,1)} %get-tuple-element.1120) | copy-start | bytes 4718596 | tf_op jit(solution)/shard_map/while
  176.3 25.1 %collective-permute-start.1 = (bf16[1,512,768]{2,1,0:T(8,128)(2,1)}, bf16[1,512,768]{2,1,0:T(8,128)(2,1)}, u32[]{:S(2)}, u32[]{:S(2)}) collective-permute-start(bf16[1,512,768]{2,1,0:T(8,128)(2,1)} %slice.85), channel_id=1, source_target_pairs={{0,1},{2,3},{4,5},{6,7},{8,9},{10,11},{12,13},{14,15},{16,17},{18,... | collective-permute-start | bytes 2359304 | tf_op jit(solution)/shard_map/while/body/eval_jaxpr/ppermute | solution.py:35
  201.5 30.2 %copy-start = (bf16[1,1024,768]{1,2,0:T(8,128)(2,1)}, bf16[1,1024,768]{1,2,0:T(8,128)(2,1)S(1)}, u32[]{:S(2)}) copy-start(bf16[1,1024,768]{1,2,0:T(8,128)(2,1)S(1)} %copy.50) | copy-start | bytes 4718596 | tf_op jit(solution)/shard_map/while
  205.2 14.5 %copy-start.3 = (pred[512,1024]{1,0:T(8,128)(4,1)S(1)}, pred[512,1024]{1,0:T(8,128)(4,1)}, u32[]{:S(2)}) copy-start(pred[512,1024]{1,0:T(8,128)(4,1)} %fusion.200) | copy-start | bytes 1572868 | tf_op jit(solution)/shard_map/while
  246.6 41.3 %copy-start.15 = (bf16[2,1,512,768]{3,2,1,0:T(8,128)(2,1)S(1)}, bf16[2,1,512,768]{3,2,1,0:T(8,128)(2,1)}, u32[]{:S(2)}) copy-start(bf16[2,1,512,768]{3,2,1,0:T(8,128)(2,1)} %get-tuple-element.1120) | copy-start | bytes 4718596 | tf_op jit(solution)/shard_map/while
  283.1 15.4 %slice-start = ((s8[4718592]{0:T(1024)(128)(4,1)}), s8[4194304]{0:T(1024)(128)(4,1)S(1)}, s32[]{:S(2)}) async-start(s8[4718592]{0:T(1024)(128)(4,1)} %bitcast.223), calls=%async_computation.13 | async-start | bytes 8388608 | tf_op jit(solution)/shard_map/while
  287.9 10.6 copy-start.61
  287.9 10.6 slice-start.1
  306.9 16.0 %copy-start.2 = (bf16[512,768]{0,1:T(8,128)(2,1)S(1)}, bf16[512,768]{0,1:T(8,128)(2,1)}, u32[]{:S(2)}) copy-start(bf16[512,768]{0,1:T(8,128)(2,1)} %copy.53) | copy-start | bytes 2359300 | tf_op jit(solution)/shard_map/while
  321.6 150.2 %collective-permute-start.2 = (bf16[1,512,768]{1,2,0:T(8,128)(2,1)}, bf16[1,512,768]{1,2,0:T(8,128)(2,1)}, u32[]{:S(2)}, u32[]{:S(2)}) collective-permute-start(bf16[1,512,768]{1,2,0:T(8,128)(2,1)} %slice.86), channel_id=1, source_target_pairs={{1,0},{3,2},{5,4},{7,6},{9,8},{11,10},{13,12},{15,14},{17,16},{19,... | collective-permute-start | bytes 2359304 | tf_op jit(solution)/shard_map/while/body/eval_jaxpr/ppermute | solution.py:35
  442.1 32.7 %collective-permute-start.3 = (bf16[1,512,768]{1,2,0:T(8,128)(2,1)}, bf16[1,512,768]{1,2,0:T(8,128)(2,1)}, u32[]{:S(2)}, u32[]{:S(2)}) collective-permute-start(bf16[1,512,768]{1,2,0:T(8,128)(2,1)} %slice.87), channel_id=1, source_target_pairs={{1,0},{3,2},{5,4},{7,6},{9,8},{11,10},{13,12},{15,14},{17,16},{19,... | collective-permute-start | bytes 2359304 | tf_op jit(solution)/shard_map/while/body/eval_jaxpr/ppermute | solution.py:35
  443.4 7.6 copy-start.17
  461.1 9.1 copy-start.7
  461.2 9.1 copy-start.18
  474.7 9.1 copy-start.38
  489.1 107.9 %copy-start.24 = (s32[1024]{0:T(1024)}, s32[1024]{0:T(1024)S(1)}, u32[]{:S(2)}) copy-start(s32[1024]{0:T(1024)S(1)} %get-tuple-element.1133) | copy-start | bytes 12292 | tf_op jit(solution)/shard_map/while
  489.1 107.9 %copy-start.44 = (pred[1024]{0:T(1024)(128)(4,1)}, pred[1024]{0:T(1024)(128)(4,1)S(1)}, u32[]{:S(2)}) copy-start(pred[1024]{0:T(1024)(128)(4,1)S(1)} %get-tuple-element.1134) | copy-start | bytes 3076 | tf_op jit(solution)/shard_map/while
  489.3 73.1 %all-gather.11.cloned.1.call-start = ((), (), s32[]{:S(2)}) async-start(), calls=%async_computation.10 | async-start | bytes 4423680 | tf_op jit(solution)/shard_map/while/body/eval_jaxpr/all_gather | solution.py:135
  489.8 154.0 %all-gather.9.cloned.1.call-start = ((), (), s32[]{:S(2)}) async-start(), calls=%async_computation.9 | async-start | bytes 1474560 | tf_op jit(solution)/shard_map/while/body/eval_jaxpr/all_gather | solution.py:138
  490.4 192.8 %all-gather.13.cloned.1.call-start = ((), (), s32[]{:S(2)}) async-start(), calls=%async_computation.11 | async-start | bytes 5898240 | tf_op jit(solution)/shard_map/while/body/eval_jaxpr/all_gather | solution.py:144
  491.2 374.3 %all-gather.15.cloned.1.call-start = ((), (), s32[]{:S(2)}) async-start(), calls=%async_computation.12 | async-start | bytes 5898240 | tf_op jit(solution)/shard_map/while/body/eval_jaxpr/all_gather | solution.py:146
  492.0 22.3 %copy-start.4 = (bf16[768,768]{1,0:T(8,128)(2,1)S(1)}, bf16[768,768]{1,0:T(8,128)(2,1)}, u32[]{:S(2)}) copy-start(bf16[768,768]{1,0:T(8,128)(2,1)} %get-tuple-element.1124) | copy-start | bytes 3538948 | tf_op jit(solution)/shard_map/while
  569.1 30.2 %collective-permute-start = (bf16[1,512,768]{2,1,0:T(8,128)(2,1)S(1)}, bf16[1,512,768]{2,1,0:T(8,128)(2,1)}, u32[]{:S(2)}, u32[]{:S(2)}) collective-permute-start(bf16[1,512,768]{2,1,0:T(8,128)(2,1)S(1)} %get-tuple-element.964), channel_id=1, source_target_pairs={{0,1},{2,3},{4,5},{6,7},{8,9},{10,11},{12,13},{14,15},{16,17},{18,... | collective-permute-start | bytes 2359304 | tf_op jit(solution)/shard_map/while/body/eval_jaxpr/ppermute | solution.py:35
  571.8 9.4 copy-start.43
  571.8 22.6 %copy-start.14 = (bf16[2,1,512,768]{3,2,1,0:T(8,128)(2,1)S(1)}, bf16[2,1,512,768]{3,2,1,0:T(8,128)(2,1)}, u32[]{:S(2)}) copy-start(bf16[2,1,512,768]{3,2,1,0:T(8,128)(2,1)} %get-tuple-element.1120) | copy-start | bytes 4718596 | tf_op jit(solution)/shard_map/while
  576.6 25.0 %collective-permute-start.1 = (bf16[1,512,768]{2,1,0:T(8,128)(2,1)}, bf16[1,512,768]{2,1,0:T(8,128)(2,1)}, u32[]{:S(2)}, u32[]{:S(2)}) collective-permute-start(bf16[1,512,768]{2,1,0:T(8,128)(2,1)} %slice.85), channel_id=1, source_target_pairs={{0,1},{2,3},{4,5},{6,7},{8,9},{10,11},{12,13},{14,15},{16,17},{18,... | collective-permute-start | bytes 2359304 | tf_op jit(solution)/shard_map/while/body/eval_jaxpr/ppermute | solution.py:35
  601.6 30.2 %copy-start = (bf16[1,1024,768]{1,2,0:T(8,128)(2,1)}, bf16[1,1024,768]{1,2,0:T(8,128)(2,1)S(1)}, u32[]{:S(2)}) copy-start(bf16[1,1024,768]{1,2,0:T(8,128)(2,1)S(1)} %copy.50) | copy-start | bytes 4718596 | tf_op jit(solution)/shard_map/while
  605.4 14.5 %copy-start.3 = (pred[512,1024]{1,0:T(8,128)(4,1)S(1)}, pred[512,1024]{1,0:T(8,128)(4,1)}, u32[]{:S(2)}) copy-start(pred[512,1024]{1,0:T(8,128)(4,1)} %fusion.200) | copy-start | bytes 1572868 | tf_op jit(solution)/shard_map/while
  646.8 41.3 %copy-start.15 = (bf16[2,1,512,768]{3,2,1,0:T(8,128)(2,1)S(1)}, bf16[2,1,512,768]{3,2,1,0:T(8,128)(2,1)}, u32[]{:S(2)}) copy-start(bf16[2,1,512,768]{3,2,1,0:T(8,128)(2,1)} %get-tuple-element.1120) | copy-start | bytes 4718596 | tf_op jit(solution)/shard_map/while
  683.2 15.4 %slice-start = ((s8[4718592]{0:T(1024)(128)(4,1)}), s8[4194304]{0:T(1024)(128)(4,1)S(1)}, s32[]{:S(2)}) async-start(s8[4718592]{0:T(1024)(128)(4,1)} %bitcast.223), calls=%async_computation.13 | async-start | bytes 8388608 | tf_op jit(solution)/shard_map/while
  688.1 10.5 copy-start.61
  688.1 10.5 slice-start.1
  707.0 16.0 %copy-start.2 = (bf16[512,768]{0,1:T(8,128)(2,1)S(1)}, bf16[512,768]{0,1:T(8,128)(2,1)}, u32[]{:S(2)}) copy-start(bf16[512,768]{0,1:T(8,128)(2,1)} %copy.53) | copy-start | bytes 2359300 | tf_op jit(solution)/shard_map/while
  721.7 154.4 %collective-permute-start.2 = (bf16[1,512,768]{1,2,0:T(8,128)(2,1)}, bf16[1,512,768]{1,2,0:T(8,128)(2,1)}, u32[]{:S(2)}, u32[]{:S(2)}) collective-permute-start(bf16[1,512,768]{1,2,0:T(8,128)(2,1)} %slice.86), channel_id=1, source_target_pairs={{1,0},{3,2},{5,4},{7,6},{9,8},{11,10},{13,12},{15,14},{17,16},{19,... | collective-permute-start | bytes 2359304 | tf_op jit(solution)/shard_map/while/body/eval_jaxpr/ppermute | solution.py:35
  842.2 36.8 %collective-permute-start.3 = (bf16[1,512,768]{1,2,0:T(8,128)(2,1)}, bf16[1,512,768]{1,2,0:T(8,128)(2,1)}, u32[]{:S(2)}, u32[]{:S(2)}) collective-permute-start(bf16[1,512,768]{1,2,0:T(8,128)(2,1)} %slice.87), channel_id=1, source_target_pairs={{1,0},{3,2},{5,4},{7,6},{9,8},{11,10},{13,12},{15,14},{17,16},{19,... | collective-permute-start | bytes 2359304 | tf_op jit(solution)/shard_map/while/body/eval_jaxpr/ppermute | solution.py:35
  843.5 9.0 copy-start.17
  865.4 9.1 copy-start.7
  865.4 9.1 copy-start.18
  879.0 11.3 copy-start.38
  880.6 9.8 copy-start.46
  898.5 33.3 %reduce-scatter.7.cloned.1.call-start = ((), (), s32[]{:S(2)}) async-start(), calls=%async_computation.5 | async-start | bytes 1474560 | tf_op jit(solution)/shard_map/reduce_scatter | solution.py:252
  901.4 97.6 %reduce-scatter.5.cloned.1.call-start = ((), (), s32[]{:S(2)}) async-start(), calls=%async_computation.4 | async-start | bytes 4423680 | tf_op jit(solution)/shard_map/reduce_scatter | solution.py:252
  906.7 179.8 %reduce-scatter.9.cloned.1.call-start = ((), (), s32[]{:S(2)}) async-start(), calls=%async_computation.6 | async-start | bytes 5898240 | tf_op jit(solution)/shard_map/reduce_scatter | solution.py:252
  913.6 261.0 %reduce-scatter.11.cloned.1.call-start = ((), (), s32[]{:S(2)}) async-start(), calls=%async_computation.7 | async-start | bytes 5898240 | tf_op jit(solution)/shard_map/reduce_scatter | solution.py:252
  920.0 254.6 %copy-start.60 = (u32[32]{0:T(128)S(1)}, u32[32]{0:T(128)}, u32[]{:S(2)}) copy-start(u32[32]{0:T(128)} %get-tuple-element.1202) | copy-start | bytes 388
  920.0 256.5 %copy-start.42 = (f32[768]{0:T(1024)S(1)}, f32[768]{0:T(1024)}, u32[]{:S(2)}) copy-start(f32[768]{0:T(1024)} %get-tuple-element.441) | copy-start | bytes 9220
  920.0 256.6 %copy-start.39 = (f32[768]{0:T(1024)S(1)}, f32[768]{0:T(1024)}, u32[]{:S(2)}) copy-start(f32[768]{0:T(1024)} %get-tuple-element.442) | copy-start | bytes 9220
  920.0 256.6 %copy-start.36 = (f32[768]{0:T(1024)S(1)}, f32[768]{0:T(1024)}, u32[]{:S(2)}) copy-start(f32[768]{0:T(1024)} %get-tuple-element.444) | copy-start | bytes 9220
  920.0 256.6 %copy-start.33 = (f32[768]{0:T(1024)S(1)}, f32[768]{0:T(1024)}, u32[]{:S(2)}) copy-start(f32[768]{0:T(1024)} %get-tuple-element.445) | copy-start | bytes 9220
  920.0 256.6 %copy-start.30 = (f32[768]{0:T(1024)S(1)}, f32[768]{0:T(1024)}, u32[]{:S(2)}) copy-start(f32[768]{0:T(1024)} %get-tuple-element.446) | copy-start | bytes 9220
  920.0 256.6 %copy-start.23 = (f32[3072]{0:T(1024)S(1)}, f32[3072]{0:T(1024)}, u32[]{:S(2)}) copy-start(f32[3072]{0:T(1024)} %get-tuple-element.450) | copy-start | bytes 36868
  920.0 333.0 %all-reduce.33.cloned.1.call-start = ((), (), s32[]{:S(2)}) async-start(), calls=%async_computation.8 | async-start | bytes 7077888 | tf_op jit(solution)/shard_map/psum | solution.py:255
  (79 other events, 273.0 us)
Sparse Core Ops, SparseCore 0:
  92.5 69.4 all-gather.10
  163.6 29.2 all-gather.8
  194.5 88.5 all-gather.12
  284.5 87.8 all-gather.14
  491.4 70.9 all-gather.10
  563.8 29.2 all-gather.8
  594.7 88.5 all-gather.12
  684.8 87.8 all-gather.14
Sparse Core Ops, SparseCore 1:
  901.9 29.9 reduce-scatter.6
  934.0 64.9 reduce-scatter.4
  1001.2 85.3 reduce-scatter.8
  1088.9 85.6 reduce-scatter.10
  1178.3 74.7 all-reduce.32
